TPU v7x, 32 devices: a whole 2x2x4 slice. The times are simulated.
32 devices in a mesh: groups: 2 (over x), gx: 16 (over z, y, core).
Axes of the slice: x: 2, y: 2, z: 4, core: 2. Of those that a mesh axis runs over, the one named last changes fastest.
Arguments:
- volume: bfloat16 [32, 256, 6, 128], P('groups', 'gx'), parts along dimension 0, may hold values from -6 to 6
- conv_weight: bfloat16 [256, 27, 128], P('gx'), may hold values from -0.078125 to 0.078125
- conv_bias: float32 [128], replicated, may hold values from -3 to 3
- tconv_weight: bfloat16 [27, 64, 128], replicated, may hold values from -0.25 to 0.25
Outputs:
- decoded: bfloat16 [64, 64, 12, 256], P(('groups', 'gx')), parts along dimension 0
There are 2 independent parts, one for each index of `groups`. A program takes and returns all parts, laid end to end along the dimension named above; an argument that names none is the same for every part. Nothing has to cross between parts.
All inputs are finite; a program needn't handle non-finite values.
Results may differ from a plain program's by a relative error of at most 0.005.
Values may be sent and summed in bfloat16 or wider, within the bound.
A program may use at most 64 MiB of HBM per device.

v0:
```python
import jax
import jax.numpy as jnp
from jax import lax
from jax.sharding import PartitionSpec as P


def extended(block, sides, width):
    for axis, dim in sides:
        count = lax.axis_size(axis)
        forward = [(i, i + 1) for i in range(count - 1)]
        backward = [(target, source) for source, target in forward]
        low = lax.ppermute(
            lax.slice_in_dim(block, block.shape[dim] - width, None, axis=dim), axis, forward
        )
        high = lax.ppermute(lax.slice_in_dim(block, 0, width, axis=dim), axis, backward)
        block = jnp.concatenate([low, block, high], axis=dim)
    return block


def from_behind(block, axis, distance):
    devices = range(lax.axis_size(axis))
    route = [(i - distance, i) for i in devices if i - distance in devices]
    return lax.ppermute(block, axis, route)


def next_cell(field, axis):
    size = field.shape[axis]
    rest = lax.slice_in_dim(field, 1, size, axis=axis)
    zero_shape = list(field.shape)
    zero_shape[axis] = 1
    return jnp.concatenate([rest, jnp.zeros(zero_shape, field.dtype)], axis=axis)


def yz_classes(products, tap_x):
    layout_options = (((1, False),), ((2, False), (0, True)))
    parity_classes = []
    for par_y in range(2):
        for par_z in range(2):
            total = jnp.zeros(products.shape[:1] + products.shape[4:], jnp.float32)
            for tap_y, shift_y in layout_options[par_y]:
                for tap_z, shift_z in layout_options[par_z]:
                    term = products[:, tap_x, tap_y, tap_z]
                    if shift_y:
                        term = next_cell(term, 2)
                    if shift_z:
                        term = next_cell(term, 3)
                    total = total + term
            parity_classes.append(total)
    return jnp.stack(parity_classes, axis=0)


def alternate(even, odd):
    both = jnp.stack([even, odd], axis=0)
    rows, chans, wide_y, wide_z = (both.shape[2], both.shape[3], both.shape[4], both.shape[5])
    both = both.reshape(2, 2, 2, rows, chans, wide_y, wide_z)
    both = jnp.transpose(both, (3, 0, 4, 5, 1, 6, 2))
    return both.reshape(2 * rows, chans, 2 * wide_y, 2 * wide_z)


def conv_rows(block, weight, count):
    chans, wide_y, wide_z = (block.shape[1], block.shape[2] - 2, block.shape[3] - 2)
    taps = []
    for tap_x in range(3):
        for tap_y in range(3):
            for tap_z in range(3):
                taps.append(
                    block[tap_x : tap_x + count, :, tap_y : tap_y + wide_y, tap_z : tap_z + wide_z]
                )
    patch_columns = jnp.stack(taps, axis=2).reshape(count, chans * 27, wide_y * wide_z)
    flattened_patches = weight.reshape(chans * 27, weight.shape[2])
    output_volume = jnp.einsum(
        "fwh,wb->fbh", patch_columns, flattened_patches, preferred_element_type=jnp.float32
    )
    return output_volume.reshape(count, weight.shape[2], wide_y, wide_z)


def tap_products(hidden, flattened_patches, cup):
    rows, wide_y, wide_z = (hidden.shape[0], hidden.shape[2], hidden.shape[3])
    products = jnp.einsum(
        "oc,ncyz->noyz", flattened_patches, hidden, preferred_element_type=jnp.float32
    )
    return products.reshape(rows, 3, 3, 3, cup, wide_y, wide_z)


def per_device(volume, conv_weight, conv_bias, tconv_weight):
    wide_x, wide_y, wide_z = (volume.shape[0], volume.shape[2], volume.shape[3])
    rows = wide_x // lax.axis_size("gx")
    cout = conv_weight.shape[2]
    local = lax.all_to_all(volume, "gx", split_axis=0, concat_axis=1, tiled=True)
    widened_volume = extended(local, (("gx", 0),), 1)
    padded_volume = jnp.pad(widened_volume, ((0, 0), (0, 0), (1, 1), (1, 1)))
    summed = conv_rows(padded_volume, lax.all_gather(conv_weight, "gx", axis=0, tiled=True), rows)
    hidden = jnp.maximum(summed + conv_bias[None, :, None, None], 0.0).astype(jnp.bfloat16)
    cup = tconv_weight.shape[1]
    flattened_patches = tconv_weight.reshape(27 * cup, cout)
    products = tap_products(hidden, flattened_patches, cup)
    first = yz_classes(products, 0)
    middle = yz_classes(products, 1)
    last = yz_classes(products, 2)
    edge = from_behind(hidden, "gx", -1)
    leading_edge = yz_classes(tap_products(edge, flattened_patches, cup), 0)
    following = jnp.concatenate([first[:, 1:], leading_edge], axis=1)
    odd = last + following
    return alternate(middle, odd).astype(jnp.bfloat16)


def solution(mesh):
    return jax.shard_map(
        per_device,
        mesh=mesh,
        in_specs=(P("groups", "gx", None, None), P("gx", None, None), P(), P()),
        out_specs=P(("groups", "gx"), None, None, None),
        check_vma=False,
    )
```

profile of v0, /device:TPU:9, one launch (start us, length us, event | category | flops | bytes accessed | tf_op | source)
XLA Modules:
  0.0 139.7 jit_solution(13895225849409607237)
XLA Ops:
  6.5 18.1 %all_to_all.12 = bf16[16,16,6,128]{3,1,2,0:T(8,128)(2,1)S(1)} all-to-all(bf16[16,16,6,128]{3,1,2,0:T(8,128)(2,1)} %param.4), channel_id=1, replica_groups=mesh['groups'=2,'gx'=16] {'gx'}, dimensions={0} | all-to-all | bytes 786432 | tf_op jit(solution)/shard_map/all_to_all | solution.py:89
  24.7 2.6 %collective-permute-start = (bf16[1,256,6,128]{3,1,2,0:T(8,128)(2,1)S(1)}, bf16[1,256,6,128]{3,1,2,0:T(8,128)(2,1)S(1)}, u32[]{:S(2)}, u32[]{:S(2)}) collective-permute-start(bf16[1,256,6,128]{3,1,2,0:T(8,128)(2,1)S(1)} %bitcast.296), channel_id=1, source_target_pairs={{0,1},{1,2},{2,3},{3,4},{4,5},{5,6},{6,7},{7,8},{8,9},{9,10},{10,1... | collective-permute-start | bytes 1179656 | tf_op jit(solution)/shard_map/ppermute | solution.py:12
  27.3 1.9 %collective-permute-start.1 = (bf16[1,256,6,128]{3,1,2,0:T(8,128)(2,1)S(1)}, bf16[1,256,6,128]{3,1,2,0:T(8,128)(2,1)S(1)}, u32[]{:S(2)}, u32[]{:S(2)}) collective-permute-start(bf16[1,256,6,128]{3,1,2,0:T(8,128)(2,1)S(1)} %bitcast.297), channel_id=1, source_target_pairs={{1,0},{2,1},{3,2},{4,3},{5,4},{6,5},{7,6},{8,7},{9,8},{10,9},{11,1... | collective-permute-start | bytes 1179656 | tf_op jit(solution)/shard_map/ppermute | solution.py:15
  29.2 2.7 %collective-permute-done = bf16[1,256,6,128]{3,1,2,0:T(8,128)(2,1)S(1)} collective-permute-done((bf16[1,256,6,128]{3,1,2,0:T(8,128)(2,1)S(1)}, bf16[1,256,6,128]{3,1,2,0:T(8,128)(2,1)S(1)}, u32[]{:S(2)}, u32[]{:S(2)}) %collective-permute-start) | collective-permute-done | bytes 393248 | tf_op jit(solution)/shard_map/ppermute | solution.py:12
  32.0 6.2 %collective-permute-done.1 = bf16[1,256,6,128]{3,1,2,0:T(8,128)(2,1)S(1)} collective-permute-done((bf16[1,256,6,128]{3,1,2,0:T(8,128)(2,1)S(1)}, bf16[1,256,6,128]{3,1,2,0:T(8,128)(2,1)S(1)}, u32[]{:S(2)}, u32[]{:S(2)}) %collective-permute-start.1) | collective-permute-done | bytes 393248 | tf_op jit(solution)/shard_map/ppermute | solution.py:15
  38.2 1.7 %select_maximum_fusion = bf16[3,256,8,130]{3,1,2,0:T(8,128)(2,1)S(1)} fusion(bf16[1,256,6,128]{3,1,2,0:T(8,128)(2,1)S(1)} %collective-permute-done.1, bf16[1,256,6,128]{3,1,2,0:T(8,128)(2,1)S(1)} %bitcast.298, bf16[1,256,6,128]{3,1,2,0:T(8,128)(2,1)S(1)} %collective-permute-done), kind=kLoop, calls=%fused_computation.8 | loop fusion | flops 15175680 | bytes 2777088 | tf_op jit(solution)/shard_map/concatenate | solution.py:16
  40.0 0.2 fusion.31
  40.2 0.2 fusion.30
  40.4 0.1 fusion.29
  40.6 0.2 fusion.28
  40.9 0.1 fusion.27
  41.0 0.2 fusion.26
  41.2 0.2 fusion.25
  41.6 0.2 fusion.23
  41.8 0.2 fusion.22
  42.2 0.2 fusion.20
  42.6 0.2 fusion.18
  42.8 0.2 fusion.17
  43.1 0.2 fusion.15
  43.4 0.2 fusion.14
  43.6 0.1 fusion.13
  43.8 0.2 fusion.12
  44.1 0.2 fusion.10
  44.4 0.2 fusion.9
  44.6 43.2 %copy.129 = bf16[1,256,27,6,128]{4,3,2,1,0:T(8,128)(2,1)S(1)} copy(bf16[1,256,27,6,128]{4,1,3,2,0:T(8,128)(2,1)S(1)} %fusion.9) | data formatting | bytes 21233664 | tf_op jit(solution)/shard_map/stack | solution.py:69
  87.8 6.4 %copy.252 = bf16[864,8,6,128]{3,1,2,0:T(8,128)(2,1)} copy(bf16[864,8,6,128]{3,2,1,0:T(8,128)(2,1)S(1)} %bitcast.288) | data formatting | bytes 21233664
  94.3 13.9 %copy.130 = bf16[768,6912]{1,0:T(8,128)(2,1)} copy(bf16[768,6912]{0,1:T(8,128)(2,1)} %bitcast.289) | data formatting | bytes 21233664 | tf_op jit(solution)/shard_map/fwh,wb->fbh/dot_general | solution.py:71
  108.1 2.7 %copy.131 = bf16[256,27,128]{2,1,0:T(8,128)(2,1)S(1)} copy(bf16[256,27,128]{2,0,1:T(8,128)(2,1)} %all-gather.2.cloned.1.call-done) | data formatting | bytes 3538944 | tf_op jit(solution)/shard_map/all_gather | solution.py:92
  110.8 1.6 %reshape.119 = bf16[6912,128,1]{1,0,2:T(8,128)(2,1)} reshape(bf16[256,27,128]{2,1,0:T(8,128)(2,1)S(1)} %copy.131) | data formatting | bytes 3538944 | tf_op jit(solution)/shard_map/reshape | solution.py:70
  112.4 7.4 %fusion.7 = bf16[6,128,128]{2,1,0:T(8,128)(2,1)S(1)} fusion(bf16[6,128,6912]{2,1,0:T(8,128)(2,1)} %bitcast.292, bf16[6912,128,1]{1,0,2:T(8,128)(2,1)} %reshape.119, f32[128]{0:T(128)S(1)} %copy-done.1), kind=kOutput, calls=%fused_computation.15 | convolution fusion | flops 1359249408 | bytes 12583424 | tf_op jit(solution)/shard_map/fwh,wb->fbh/dot_general | solution.py:71
  119.8 0.9 fusion.59
  120.7 0.4 fusion.65
  121.2 0.1 slice.310
  121.3 0.1 slice.316
  121.5 0.1 pad_slice_fusion.2
  121.6 1.9 %collective-permute-start.2 = (bf16[1,128,6,128]{1,3,2,0:T(8,128)(2,1)S(1)}, bf16[1,128,6,128]{1,3,2,0:T(8,128)(2,1)S(1)}, u32[]{:S(2)}, u32[]{:S(2)}) collective-permute-start(bf16[1,128,6,128]{1,3,2,0:T(8,128)(2,1)S(1)} %bitcast.303), channel_id=1, source_target_pairs={{1,0},{2,1},{3,2},{4,3},{5,4},{6,5},{7,6},{8,7},{9,8},{10,9},{11,1... | collective-permute-start | bytes 589832 | tf_op jit(solution)/shard_map/ppermute | solution.py:23
  123.6 0.1 slice.324
  123.7 0.1 slice.330
  123.9 0.1 pad_slice_fusion.1
  124.4 4.3 %collective-permute-done.2 = bf16[1,128,6,128]{1,3,2,0:T(8,128)(2,1)S(1)} collective-permute-done((bf16[1,128,6,128]{1,3,2,0:T(8,128)(2,1)S(1)}, bf16[1,128,6,128]{1,3,2,0:T(8,128)(2,1)S(1)}, u32[]{:S(2)}, u32[]{:S(2)}) %collective-permute-start.2) | collective-permute-done | bytes 196640 | tf_op jit(solution)/shard_map/ppermute | solution.py:23
  128.6 0.9 fusion.57
  129.6 0.1 pad_slice_fusion
  129.7 0.1 slice.338
  129.8 0.1 slice.344
  130.0 0.1 fusion.56
  130.1 0.1 fusion.8
  130.3 1.2 copy.161
  131.5 1.4 %copy.162 = bf16[2,64,12,256]{3,1,2,0:T(8,128)(2,1)} copy(bf16[2,64,12,256]{1,3,2,0:T(8,128)(2,1)S(1)} %bitcast.295) | data formatting | bytes 1572864 | tf_op jit(solution)/shard_map/convert_element_type | solution.py:104
  (42 shorter events, 1.5 us)
Async XLA Ops:
  6.5 113.3 %copy-start = (bf16[27,64,128]{2,1,0:T(8,128)(2,1)S(1)}, bf16[27,64,128]{2,1,0:T(8,128)(2,1)}, u32[]{:S(2)}) copy-start(bf16[27,64,128]{2,1,0:T(8,128)(2,1)} %param.7) | copy-start | bytes 1327108
  6.5 101.6 %all-gather.2.cloned.1.call-start = ((), (), s32[]{:S(2)}) async-start(), calls=%async_computation.1 | async-start | bytes 1880064 | tf_op jit(solution)/shard_map/all_gather | solution.py:92
  24.7 7.3 %collective-permute-start = (bf16[1,256,6,128]{3,1,2,0:T(8,128)(2,1)S(1)}, bf16[1,256,6,128]{3,1,2,0:T(8,128)(2,1)S(1)}, u32[]{:S(2)}, u32[]{:S(2)}) collective-permute-start(bf16[1,256,6,128]{3,1,2,0:T(8,128)(2,1)S(1)} %bitcast.296), channel_id=1, source_target_pairs={{0,1},{1,2},{2,3},{3,4},{4,5},{5,6},{6,7},{7,8},{8,9},{9,10},{10,1... | collective-permute-start | bytes 1179656 | tf_op jit(solution)/shard_map/ppermute | solution.py:12
  27.3 10.9 %collective-permute-start.1 = (bf16[1,256,6,128]{3,1,2,0:T(8,128)(2,1)S(1)}, bf16[1,256,6,128]{3,1,2,0:T(8,128)(2,1)S(1)}, u32[]{:S(2)}, u32[]{:S(2)}) collective-permute-start(bf16[1,256,6,128]{3,1,2,0:T(8,128)(2,1)S(1)} %bitcast.297), channel_id=1, source_target_pairs={{1,0},{2,1},{3,2},{4,3},{5,4},{6,5},{7,6},{8,7},{9,8},{10,9},{11,1... | collective-permute-start | bytes 1179656 | tf_op jit(solution)/shard_map/ppermute | solution.py:15
  94.3 18.1 %copy-start.1 = (f32[128]{0:T(128)S(1)}, f32[128]{0:T(128)}, u32[]{:S(2)}) copy-start(f32[128]{0:T(128)} %param.6) | copy-start | bytes 1540
  121.6 7.0 %collective-permute-start.2 = (bf16[1,128,6,128]{1,3,2,0:T(8,128)(2,1)S(1)}, bf16[1,128,6,128]{1,3,2,0:T(8,128)(2,1)S(1)}, u32[]{:S(2)}, u32[]{:S(2)}) collective-permute-start(bf16[1,128,6,128]{1,3,2,0:T(8,128)(2,1)S(1)} %bitcast.303), channel_id=1, source_target_pairs={{1,0},{2,1},{3,2},{4,3},{5,4},{6,5},{7,6},{8,7},{9,8},{10,9},{11,1... | collective-permute-start | bytes 589832 | tf_op jit(solution)/shard_map/ppermute | solution.py:23
Sparse Core Ops, SparseCore 0:
  29.3 40.2 all-gather.1
where the time goes:
time: 141 us; the launch traced here: 140 us
  local copies, waits for them, and re-layouts  76.6 us (54%)
  blocking collectives  18.1 us (13%)
  between operations  13.9 us (10%)
  waiting for transfers between devices  13.2 us (9%)
  matrix products  9.14 us (6%)
  starting transfers between devices  6.4 us (5%)
  other arithmetic  2.26 us (2%)
    another operation x2, local copies, waits for them, and re-layouts, conv_rows(): jnp.stack(taps, axis=2).reshape(count, chans * 27, wide_y * wide_z)  43.4 us
    all_to_all x1, blocking collectives, per_device(): lax.all_to_all(volume, 'gx', split_axis=0, concat_axis=1, tiled=True)  18.1 us
    dot_general x1, local copies, waits for them, and re-layouts, conv_rows(): jnp.einsum('fwh,wb->fbh', patch_columns, flattened_patches, preferred_ele...  13.9 us
    unnamed x32, local copies, waits for them, and re-layouts  10.8 us
    dot_general x1, matrix products, conv_rows(): jnp.einsum('fwh,wb->fbh', patch_columns, flattened_patches, preferred_ele...  7.43 us
    ppermute x1, waiting for transfers between devices, extended(): lax.ppermute(lax.slice_in_dim(block, 0, width, axis=dim), axis, backward)  6.21 us
    ppermute x1, waiting for transfers between devices, from_behind(): return lax.ppermute(block, axis, route)  4.26 us
  transfers between devices with their start and end apart: 4, of which 3 were waited for; matrix products, arithmetic and copies ran while one was open for 50% of the time, Pallas kernels for 0%

commit v1 on v0

v1 whole, which is shorter than its diff:
```python
import jax
import jax.numpy as jnp
from jax import lax
from jax.experimental import pallas as pl
from jax.experimental.pallas import tpu as pltpu
from jax.sharding import PartitionSpec as P

MESH = pl.DeviceIdType.MESH
VMEM = pl.BlockSpec(memory_space=pltpu.VMEM)
ANY = pl.BlockSpec(memory_space=pl.ANY)


def shift_up(block):
    lane = lax.broadcasted_iota(jnp.int32, block.shape, 1)
    return jnp.where(lane == 0, 0.0, pltpu.roll(block, 1, axis=1))


def shift_down(block):
    size = block.shape[1]
    lane = lax.broadcasted_iota(jnp.int32, block.shape, 1)
    return jnp.where(lane == size - 1, 0.0, pltpu.roll(block, size - 1, axis=1))


def conv_hidden(planes, wide_y, wide_z, tap, bias):
    zero = jnp.zeros_like(planes[0](0))
    total = None
    for kx in range(3):
        padded = jnp.concatenate(
            [zero] + [planes[kx](y) for y in range(wide_y)] + [zero], axis=1
        )
        for ky in range(3):
            weight = jnp.concatenate([tap(kx * 9 + ky * 3 + kz) for kz in range(3)], axis=1)
            cells = padded[:, ky * wide_z : (ky + wide_y) * wide_z]
            term = lax.dot_general(
                weight, cells, (((0,), (0,)), ((), ())), preferred_element_type=jnp.float32
            )
            total = term if total is None else total + term
    cout = total.shape[0] // 3
    rows = []
    for y in range(wide_y):
        part = total[:, y * wide_z : (y + 1) * wide_z]
        rows.append(
            part[cout : 2 * cout]
            + shift_up(part[:cout])
            + shift_down(part[2 * cout :])
        )
    summed = jnp.concatenate(rows, axis=1)
    return jnp.maximum(summed + bias, 0.0).astype(jnp.bfloat16)


def exchange_conv(volume, weight, bias, hidden_out, planes, weights, hidden, entry_sem,
                  vsend, vrecv, hsend, hrecv, wsend, wrecv, xsend, csend, crecv, esend, erecv):
    me = lax.axis_index("gx")
    count = lax.axis_size("gx")
    group = lax.axis_index("groups")
    chips = count // 2
    chip, core = me // 2, me % 2
    wide_y, wide_z = volume.shape[1], volume.shape[3]

    barrier = pltpu.get_barrier_semaphore()
    for d in range(1, count):
        pl.semaphore_signal(
            barrier, inc=1, device_id={"gx": (me + d) % count}, device_id_type=MESH
        )
    pl.semaphore_signal(barrier, inc=1, device_id={"groups": 1 - group}, device_id_type=MESH)
    pl.semaphore_wait(barrier, count)

    def remote(src, dst, send, recv, target):
        return pltpu.make_async_remote_copy(
            src_ref=src, dst_ref=dst, send_sem=send, recv_sem=recv,
            device_id=target, device_id_type=MESH,
        )

    own_volume = pltpu.make_async_copy(volume.at[me], planes.at[1, me], entry_sem.at[0])
    own_weight = pltpu.make_async_copy(weight, weights.at[me], entry_sem.at[1])
    own_volume.start()
    own_weight.start()

    def piece(d):
        to = (me + d) % count
        return remote(volume.at[to], planes.at[1, me], vsend.at[d], vrecv.at[d], {"gx": to})

    order = [d for pair in zip(range(1, count // 2), range(count - 1, count // 2, -1)) for d in pair]
    order.append(count // 2)
    for d in order:
        piece(d).start()

    def source(k):
        return (chip + chips - k) % chips

    def leads(c):
        return (c // 2 + c) % 2 == group

    def direct(k):
        to = ((chip + k) % chips) * 2 + core
        return remote(weight, weights.at[me], wsend.at[k], wrecv.at[k], {"gx": to})

    def across(k):
        at = weights.at[source(k) * 2 + core]
        return remote(at, at, xsend.at[k], wrecv.at[k], {"groups": 1 - group})

    def beside(k):
        slot = source(k) * 2 + core
        src = weight if k == 0 else weights.at[slot]
        return remote(src, weights.at[slot], csend.at[k], crecv.at[k], {"gx": chip * 2 + 1 - core})

    def beside_arrival(k):
        slot = source(k) * 2 + 1 - core
        at = weights.at[slot]
        return remote(at, at, csend.at[k], crecv.at[k], {"gx": chip * 2 + 1 - core})

    beside(0).start()

    @pl.when(leads(chip))
    def _():
        for k in range(1, chips):
            direct(k).start()

    @pl.when(me == 0)
    def _():
        planes[0] = jnp.zeros(planes.shape[1:], planes.dtype)

    @pl.when(me == count - 1)
    def _():
        planes[2] = jnp.zeros(planes.shape[1:], planes.dtype)
        hidden[1] = jnp.zeros(hidden.shape[1:], hidden.dtype)

    def arrived(at, sem):
        pltpu.make_async_copy(at, at, sem).wait()

    own_volume.wait()
    for d in order:
        arrived(planes.at[1, (me + count - d) % count], vrecv.at[d])

    def to_right():
        return remote(planes.at[1], planes.at[0], hsend.at[0], hrecv.at[0], {"gx": me + 1})

    def to_left():
        return remote(planes.at[1], planes.at[2], hsend.at[1], hrecv.at[1], {"gx": me - 1})

    @pl.when(me < count - 1)
    def _():
        to_right().start()

    @pl.when(me > 0)
    def _():
        to_left().start()

    for wanted in (True, False):
        for k in range(1, chips):
            @pl.when(leads(source(k)) == wanted)
            def _(k=k, wanted=wanted):
                arrived(weights.at[source(k) * 2 + core], wrecv.at[k])
                if wanted:
                    across(k).start()
                beside(k).start()

    own_weight.wait()
    for k in range(chips):
        arrived(weights.at[source(k) * 2 + 1 - core], crecv.at[k])

    @pl.when(me > 0)
    def _():
        arrived(planes.at[0], hrecv.at[0])

    @pl.when(me < count - 1)
    def _():
        arrived(planes.at[2], hrecv.at[1])

    cin = count * volume.shape[2]
    cells = [lambda y, kx=kx: planes[kx, :, y].reshape(cin, wide_z) for kx in range(3)]
    hidden[0] = conv_hidden(
        cells, wide_y, wide_z, lambda t: weights[:, t].reshape(cin, weights.shape[3]), bias[...]
    )

    def edge():
        return remote(hidden.at[0], hidden.at[1], esend, erecv, {"gx": me - 1})

    @pl.when(me > 0)
    def _():
        edge().start()

    for d in order:
        piece(d).wait_send()

    @pl.when(leads(chip))
    def _():
        for k in range(1, chips):
            direct(k).wait_send()

    for k in range(1, chips):
        @pl.when(leads(source(k)))
        def _(k=k):
            across(k).wait_send()

    for k in range(chips):
        beside(k).wait_send()

    @pl.when(me < count - 1)
    def _():
        to_right().wait_send()

    @pl.when(me > 0)
    def _():
        to_left().wait_send()

    @pl.when(me < count - 1)
    def _():
        arrived(hidden.at[1], erecv)

    @pl.when(me > 0)
    def _():
        edge().wait_send()

    hidden_out[...] = hidden[...]


def local_conv(planes, weight, bias, hidden_out):
    wide_y, wide_z = planes.shape[1], planes.shape[3]
    cells = [lambda y, kx=kx: planes[kx, y] for kx in range(3)]
    hidden_out[...] = conv_hidden(cells, wide_y, wide_z, lambda t: weight[t], bias[...])


def transposed(hidden, tconv, out):
    wide_z = out.shape[3] // 2
    wide_y = out.shape[1] // 2
    cup = tconv.shape[1]
    cout = tconv.shape[2]
    here, after = hidden[0], hidden[1]

    def down(x):
        return jnp.concatenate([x[:, wide_z:], jnp.zeros_like(x[:, :wide_z])], axis=1)

    def taps(kx, ky):
        t = kx * 9 + ky * 3
        return tconv[t : t + 3].reshape(3 * cup, cout)

    row = lax.broadcasted_iota(jnp.int32, (2 * wide_z, 2 * wide_z), 0)
    col = lax.broadcasted_iota(jnp.int32, (2 * wide_z, 2 * wide_z), 1)
    spread = jnp.where(
        col == jnp.where(row < wide_z, 2 * row, 2 * (row - wide_z) + 1), 1.0, 0.0
    ).astype(jnp.bfloat16)
    x_options = (((1, here),), ((2, here), (0, after)))
    for pu in range(2):
        for pv in range(2):
            left, right = [], []
            for kx, field in x_options[pu]:
                for ky, shifted in (((1, False),), ((2, False), (0, True)))[pv]:
                    left.append(taps(kx, ky))
                    right.append(down(field) if shifted else field)
            product = jnp.dot(
                jnp.concatenate(left, axis=1), jnp.concatenate(right, axis=0),
                preferred_element_type=jnp.float32,
            )
            pairs = []
            for y in range(wide_y):
                part = product[:, y * wide_z : (y + 1) * wide_z]
                even = part[cup : 2 * cup]
                odd = part[2 * cup :] + shift_down(part[:cup])
                pairs.append(jnp.concatenate([even, odd], axis=1).astype(jnp.bfloat16))
            mixed = jnp.dot(
                jnp.concatenate(pairs, axis=0), spread, preferred_element_type=jnp.float32
            ).astype(jnp.bfloat16)
            for y in range(wide_y):
                out[pu, 2 * y + pv] = mixed[y * cup : (y + 1) * cup]


def native_hidden(volume, conv_weight, bias):
    count = lax.axis_size("gx")
    forward = [(i, i + 1) for i in range(count - 1)]
    backward = [(i + 1, i) for i in range(count - 1)]
    local = lax.all_to_all(volume, "gx", split_axis=0, concat_axis=1, tiled=True)
    weight = lax.all_gather(conv_weight, "gx", axis=0, tiled=True)
    rows = local.shape[0]
    low = lax.ppermute(local[rows - 1 :], "gx", forward)
    high = lax.ppermute(local[:1], "gx", backward)
    planes = jnp.transpose(jnp.concatenate([low, local, high], axis=0), (0, 2, 1, 3))
    weight = jnp.transpose(weight, (1, 0, 2))
    cout = weight.shape[2]
    shape = jax.ShapeDtypeStruct((cout, planes.shape[1] * planes.shape[3]), jnp.bfloat16)
    conv = pl.pallas_call(
        local_conv, out_shape=shape, in_specs=[VMEM] * 3, out_specs=VMEM,
        compiler_params=pltpu.CompilerParams(vmem_limit_bytes=40 << 20),
    )
    hidden = [conv(planes[r : r + 3], weight, bias) for r in range(rows)]
    hidden.append(lax.ppermute(hidden[0], "gx", backward))
    return [jnp.stack(hidden[r : r + 2]) for r in range(rows)]


def remote_hidden(volume, conv_weight, bias):
    count = lax.axis_size("gx")
    chips = count // 2
    cells = jnp.transpose(volume, (0, 2, 1, 3))
    weight = jnp.transpose(conv_weight, (1, 0, 2))
    cout = weight.shape[2]
    lanes = cells.shape[1] * cells.shape[3]
    dma = pltpu.SemaphoreType.DMA
    hidden = pl.pallas_call(
        exchange_conv,
        out_shape=jax.ShapeDtypeStruct((2, cout, lanes), jnp.bfloat16),
        in_specs=[ANY, ANY, VMEM],
        out_specs=VMEM,
        scratch_shapes=[
            pltpu.VMEM((3, count) + cells.shape[1:], jnp.bfloat16),
            pltpu.VMEM((count,) + weight.shape, jnp.bfloat16),
            pltpu.VMEM((2, cout, lanes), jnp.bfloat16),
            dma((2,)),
            dma((count,)), dma((count,)),
            dma((2,)), dma((2,)),
            dma((chips,)), dma((chips,)), dma((chips,)),
            dma((chips,)), dma((chips,)),
            dma(()), dma(()),
        ],
        compiler_params=pltpu.CompilerParams(
            collective_id=0, has_side_effects=True, vmem_limit_bytes=40 << 20
        ),
    )(cells, weight, bias)
    return [hidden]


def per_device(volume, conv_weight, conv_bias, tconv_weight):
    count = lax.axis_size("gx")
    rows = volume.shape[0] // count
    bias = conv_bias[:, None]
    suited = (
        rows == 1 and count == 16 and lax.axis_size("groups") == 2
        and volume.shape[1] % 16 == 0
    )
    hidden = (remote_hidden if suited else native_hidden)(volume, conv_weight, bias)
    cup = tconv_weight.shape[1]
    shape = jax.ShapeDtypeStruct(
        (2, 2 * volume.shape[2], cup, 2 * volume.shape[3]), jnp.bfloat16
    )
    tconv = pl.pallas_call(
        transposed, out_shape=shape, in_specs=[VMEM] * 2, out_specs=VMEM,
        compiler_params=pltpu.CompilerParams(vmem_limit_bytes=40 << 20),
    )
    outs = [tconv(planes, tconv_weight) for planes in hidden]
    out = outs[0] if len(outs) == 1 else jnp.concatenate(outs, axis=0)
    return jnp.transpose(out, (0, 2, 1, 3))


def solution(mesh):
    return jax.shard_map(
        per_device,
        mesh=mesh,
        in_specs=(P("groups", "gx", None, None), P("gx", None, None), P(), P()),
        out_specs=P(("groups", "gx"), None, None, None),
        check_vma=False,
    )
```

time: 141 us -> 46.7 us (0.33)
  the two profiles are of different devices: /device:TPU:9 before, /device:TPU:0 now
where the time goes in v1:
time: 46.7 us; the launch traced here: 46.5 us
  Pallas kernels  43.8 us (94%)
  local copies, waits for them, and re-layouts  2.66 us (6%)
    pallas_call x1, Pallas kernels, remote_hidden(): pl.pallas_call(exchange_conv, out_shape=jax.ShapeDtypeStruct((2, cout, la...  41.7 us
    unnamed x8, local copies, waits for them, and re-layouts  2.55 us
    pallas_call x1, Pallas kernels, per_device(): outs = [tconv(planes, tconv_weight) for planes in hidden]  2.09 us

profile of v1, /device:TPU:0, one launch (start us, length us, event | category | flops | bytes accessed | tf_op | source)
XLA Modules:
  0.0 46.5 jit_solution(18096030398188767707)
XLA Ops:
  0.0 0.0 copy-start.3
  0.0 0.7 %copy-done.3 = f32[128]{0:T(128)S(1)} copy-done((f32[128]{0:T(128)S(1)}, f32[128]{0:T(128)}, u32[]{:S(2)}) %copy-start.3) | copy-done | bytes 536
  0.7 0.1 copy.5.bias
  0.8 0.0 copy-start.1
  0.8 1.0 %copy-done.1 = bf16[16,16,6,128]{3,1,2,0:T(8,128)(2,1)S(1)} copy-done((bf16[16,16,6,128]{3,1,2,0:T(8,128)(2,1)S(1)}, bf16[16,16,6,128]{3,1,2,0:T(8,128)(2,1)}, u32[]{:S(2)}) %copy-start.1) | copy-done | bytes 393240
  1.8 0.0 copy-start.2
  1.8 0.9 %copy-done.2 = bf16[16,27,128]{2,0,1:T(8,128)(2,1)S(1)} copy-done((bf16[16,27,128]{2,0,1:T(8,128)(2,1)S(1)}, bf16[16,27,128]{2,0,1:T(8,128)(2,1)}, u32[]{:S(2)}) %copy-start.2) | copy-done | bytes 110616
  2.7 0.0 copy-start
  2.7 41.7 %shard_map.46.hidden = bf16[2,128,768]{2,1,0:T(8,128)(2,1)S(1)} custom-call(bf16[16,6,16,128]{3,2,1,0:T(8,128)(2,1)S(1)} %bitcast.4, bf16[27,16,128]{2,1,0:T(8,128)(2,1)S(1)} %bitcast.5, f32[128,1]{1,0:T(8,128)S(1)} %copy.5.bias), custom_call_target="tpu_custom_call" | custom-call | tf_op jit(solution)/shard_map/pallas_call | solution.py:298
  44.4 0.0 copy-done
  44.4 2.1 %shard_map.47 = bf16[2,12,64,256]{3,2,1,0:T(8,128)(2,1)} custom-call(bf16[2,128,768]{2,1,0:T(8,128)(2,1)S(1)} %shard_map.46.hidden, bf16[27,64,128]{2,1,0:T(8,128)(2,1)S(1)} %copy-done), custom_call_target="tpu_custom_call" | custom-call | tf_op jit(solution)/shard_map/pallas_call | solution.py:338
Async XLA Ops:
  0.0 0.7 %copy-start.3 = (f32[128]{0:T(128)S(1)}, f32[128]{0:T(128)}, u32[]{:S(2)}) copy-start(f32[128]{0:T(128)} %param.6) | copy-start | bytes 1540
  0.8 1.0 %copy-start.1 = (bf16[16,16,6,128]{3,1,2,0:T(8,128)(2,1)S(1)}, bf16[16,16,6,128]{3,1,2,0:T(8,128)(2,1)}, u32[]{:S(2)}) copy-start(bf16[16,16,6,128]{3,1,2,0:T(8,128)(2,1)} %param.4) | copy-start | bytes 1179652
  1.8 0.9 %copy-start.2 = (bf16[16,27,128]{2,0,1:T(8,128)(2,1)S(1)}, bf16[16,27,128]{2,0,1:T(8,128)(2,1)}, u32[]{:S(2)}) copy-start(bf16[16,27,128]{2,0,1:T(8,128)(2,1)} %param.5) | copy-start | bytes 331780
  2.7 41.8 %copy-start = (bf16[27,64,128]{2,1,0:T(8,128)(2,1)S(1)}, bf16[27,64,128]{2,1,0:T(8,128)(2,1)}, u32[]{:S(2)}) copy-start(bf16[27,64,128]{2,1,0:T(8,128)(2,1)} %tconv.1) | copy-start | bytes 1327108

commit v2 on v1

--- a/solution.py
+++ b/solution.py
@@ -7,7 +7,7 @@
 
 MESH = pl.DeviceIdType.MESH
 VMEM = pl.BlockSpec(memory_space=pltpu.VMEM)
-ANY = pl.BlockSpec(memory_space=pl.ANY)
+HBM = pl.BlockSpec(memory_space=pltpu.HBM)
 
 
 def shift_up(block):
@@ -43,13 +43,13 @@
             part[cout : 2 * cout]
             + shift_up(part[:cout])
             + shift_down(part[2 * cout :])
+            + bias
         )
-    summed = jnp.concatenate(rows, axis=1)
-    return jnp.maximum(summed + bias, 0.0).astype(jnp.bfloat16)
-
-
-def exchange_conv(volume, weight, bias, hidden_out, planes, weights, hidden, entry_sem,
-                  vsend, vrecv, hsend, hrecv, wsend, wrecv, xsend, csend, crecv, esend, erecv):
+    return jnp.maximum(jnp.concatenate(rows, axis=1), 0.0).astype(jnp.bfloat16)
+
+
+def exchange_conv(volume, weight, bias, hidden_out, planes, weights, hidden, bias_row, entry_sem,
+                  vsend, vrecv, hsend, hrecv, wsend, rsend, wrecv, xsend, csend, crecv, esend, erecv):
     me = lax.axis_index("gx")
     count = lax.axis_size("gx")
     group = lax.axis_index("groups")
@@ -73,48 +73,61 @@
 
     own_volume = pltpu.make_async_copy(volume.at[me], planes.at[1, me], entry_sem.at[0])
     own_weight = pltpu.make_async_copy(weight, weights.at[me], entry_sem.at[1])
-    own_volume.start()
-    own_weight.start()
+    own_bias = pltpu.make_async_copy(bias, bias_row, entry_sem.at[2])
+
+    half = chips // 2
+    place = chip % half
+    base = chip - place
+    mirror = (chip + half) % chips
+
+    def near(j):
+        return base + (place + j) % half
+
+    def far(j):
+        return (half - base) + (place + j) % half
+
+    def leads(c):
+        return (c // 2 + c) % 2 == group
+
+    def direct(j):
+        to = mirror if j == 0 else near(j)
+        return remote(weight, weights.at[me], wsend.at[j], wrecv.at[chip], {"gx": to * 2 + core})
+
+    def relay(j):
+        at = weights.at[mirror * 2 + core]
+        return remote(at, at, rsend.at[j], wrecv.at[mirror], {"gx": near(j) * 2 + core})
+
+    def across(c):
+        at = weights.at[c * 2 + core]
+        return remote(at, at, xsend.at[c], wrecv.at[c], {"groups": 1 - group})
+
+    def beside(c, own=False):
+        slot = c * 2 + core
+        src = weight if own else weights.at[slot]
+        return remote(src, weights.at[slot], csend.at[c], crecv.at[c], {"gx": chip * 2 + 1 - core})
 
     def piece(d):
         to = (me + d) % count
         return remote(volume.at[to], planes.at[1, me], vsend.at[d], vrecv.at[d], {"gx": to})
 
+    def arrived(at, sem):
+        pltpu.make_async_copy(at, at, sem).wait()
+
     order = [d for pair in zip(range(1, count // 2), range(count - 1, count // 2, -1)) for d in pair]
-    order.append(count // 2)
+    order = [count // 2] + order[::-1]
+    others = [mirror] + [near(j) for j in range(1, half)] + [far(j) for j in range(1, half)]
+
+    @pl.when(leads(chip))
+    def _():
+        for j in range(half):
+            direct(j).start()
+
     for d in order:
         piece(d).start()
-
-    def source(k):
-        return (chip + chips - k) % chips
-
-    def leads(c):
-        return (c // 2 + c) % 2 == group
-
-    def direct(k):
-        to = ((chip + k) % chips) * 2 + core
-        return remote(weight, weights.at[me], wsend.at[k], wrecv.at[k], {"gx": to})
-
-    def across(k):
-        at = weights.at[source(k) * 2 + core]
-        return remote(at, at, xsend.at[k], wrecv.at[k], {"groups": 1 - group})
-
-    def beside(k):
-        slot = source(k) * 2 + core
-        src = weight if k == 0 else weights.at[slot]
-        return remote(src, weights.at[slot], csend.at[k], crecv.at[k], {"gx": chip * 2 + 1 - core})
-
-    def beside_arrival(k):
-        slot = source(k) * 2 + 1 - core
-        at = weights.at[slot]
-        return remote(at, at, csend.at[k], crecv.at[k], {"gx": chip * 2 + 1 - core})
-
-    beside(0).start()
-
-    @pl.when(leads(chip))
-    def _():
-        for k in range(1, chips):
-            direct(k).start()
+    beside(chip, True).start()
+    own_volume.start()
+    own_weight.start()
+    own_bias.start()
 
     @pl.when(me == 0)
     def _():
@@ -125,8 +138,15 @@
         planes[2] = jnp.zeros(planes.shape[1:], planes.dtype)
         hidden[1] = jnp.zeros(hidden.shape[1:], hidden.dtype)
 
-    def arrived(at, sem):
-        pltpu.make_async_copy(at, at, sem).wait()
+    for c in others:
+        @pl.when(leads(c))
+        def _(c=c):
+            arrived(weights.at[c * 2 + core], wrecv.at[c])
+            if c is mirror:
+                for j in range(1, half):
+                    relay(j).start()
+            across(c).start()
+            beside(c).start()
 
     own_volume.wait()
     for d in order:
@@ -146,18 +166,16 @@
     def _():
         to_left().start()
 
-    for wanted in (True, False):
-        for k in range(1, chips):
-            @pl.when(leads(source(k)) == wanted)
-            def _(k=k, wanted=wanted):
-                arrived(weights.at[source(k) * 2 + core], wrecv.at[k])
-                if wanted:
-                    across(k).start()
-                beside(k).start()
+    for c in others:
+        @pl.when(jnp.logical_not(leads(c)))
+        def _(c=c):
+            arrived(weights.at[c * 2 + core], wrecv.at[c])
+            beside(c).start()
 
     own_weight.wait()
-    for k in range(chips):
-        arrived(weights.at[source(k) * 2 + 1 - core], crecv.at[k])
+    own_bias.wait()
+    for c in [chip] + others:
+        arrived(weights.at[c * 2 + 1 - core], crecv.at[c])
 
     @pl.when(me > 0)
     def _():
@@ -170,7 +188,8 @@
     cin = count * volume.shape[2]
     cells = [lambda y, kx=kx: planes[kx, :, y].reshape(cin, wide_z) for kx in range(3)]
     hidden[0] = conv_hidden(
-        cells, wide_y, wide_z, lambda t: weights[:, t].reshape(cin, weights.shape[3]), bias[...]
+        cells, wide_y, wide_z, lambda t: weights[:, t].reshape(cin, weights.shape[3]),
+        jnp.transpose(jnp.broadcast_to(bias_row[...], (wide_z, bias_row.shape[1]))),
     )
 
     def edge():
@@ -185,16 +204,18 @@
 
     @pl.when(leads(chip))
     def _():
-        for k in range(1, chips):
-            direct(k).wait_send()
-
-    for k in range(1, chips):
-        @pl.when(leads(source(k)))
-        def _(k=k):
-            across(k).wait_send()
-
-    for k in range(chips):
-        beside(k).wait_send()
+        for j in range(half):
+            direct(j).wait_send()
+        for j in range(1, half):
+            relay(j).wait_send()
+
+    beside(chip, True).wait_send()
+    for c in others:
+        @pl.when(leads(c))
+        def _(c=c):
+            across(c).wait_send()
+
+        beside(c).wait_send()
 
     @pl.when(me < count - 1)
     def _():
@@ -298,23 +319,24 @@
     hidden = pl.pallas_call(
         exchange_conv,
         out_shape=jax.ShapeDtypeStruct((2, cout, lanes), jnp.bfloat16),
-        in_specs=[ANY, ANY, VMEM],
+        in_specs=[HBM, HBM, HBM],
         out_specs=VMEM,
         scratch_shapes=[
             pltpu.VMEM((3, count) + cells.shape[1:], jnp.bfloat16),
             pltpu.VMEM((count,) + weight.shape, jnp.bfloat16),
             pltpu.VMEM((2, cout, lanes), jnp.bfloat16),
-            dma((2,)),
+            pltpu.VMEM((1, cout), jnp.float32),
+            dma((3,)),
             dma((count,)), dma((count,)),
             dma((2,)), dma((2,)),
             dma((chips,)), dma((chips,)), dma((chips,)),
-            dma((chips,)), dma((chips,)),
+            dma((chips,)), dma((chips,)), dma((chips,)),
             dma(()), dma(()),
         ],
         compiler_params=pltpu.CompilerParams(
             collective_id=0, has_side_effects=True, vmem_limit_bytes=40 << 20
         ),
-    )(cells, weight, bias)
+    )(cells, weight, bias.reshape(1, cout))
     return [hidden]
 
 

time: 46.7 us -> 45.1 us (0.966)
  the two profiles are of different devices: /device:TPU:0 before, /device:TPU:9 now
where the time goes in v2:
time: 45.1 us; the launch traced here: 44.9 us
  Pallas kernels  42.3 us (94%)
  local copies, waits for them, and re-layouts  2.55 us (6%)
    pallas_call x1, Pallas kernels, remote_hidden(): pl.pallas_call(exchange_conv, out_shape=jax.ShapeDtypeStruct((2, cout, la...  40.2 us
    unnamed x8, local copies, waits for them, and re-layouts  2.55 us
    pallas_call x1, Pallas kernels, per_device(): outs = [tconv(planes, tconv_weight) for planes in hidden]  2.09 us

profile of v2, /device:TPU:9, one launch (start us, length us, event | category | flops | bytes accessed | tf_op | source)
XLA Modules:
  0.0 44.9 jit_solution(11459956511655548523)
XLA Ops:
  0.0 0.0 copy-start.3
  0.0 0.7 %copy-done.3 = f32[128]{0:T(128)S(1)} copy-done((f32[128]{0:T(128)S(1)}, f32[128]{0:T(128)}, u32[]{:S(2)}) %copy-start.3) | copy-done | bytes 536
  0.7 0.0 copy-start.1
  0.7 1.0 %copy-done.1 = bf16[16,16,6,128]{3,1,2,0:T(8,128)(2,1)S(1)} copy-done((bf16[16,16,6,128]{3,1,2,0:T(8,128)(2,1)S(1)}, bf16[16,16,6,128]{3,1,2,0:T(8,128)(2,1)}, u32[]{:S(2)}) %copy-start.1) | copy-done | bytes 393240
  1.7 0.0 copy-start.2
  1.7 0.9 %copy-done.2 = bf16[16,27,128]{2,0,1:T(8,128)(2,1)S(1)} copy-done((bf16[16,27,128]{2,0,1:T(8,128)(2,1)S(1)}, bf16[16,27,128]{2,0,1:T(8,128)(2,1)}, u32[]{:S(2)}) %copy-start.2) | copy-done | bytes 110616
  2.5 0.0 copy-start
  2.6 40.2 %shard_map.46.hidden = bf16[2,128,768]{2,1,0:T(8,128)(2,1)S(1)} custom-call(bf16[16,6,16,128]{3,2,1,0:T(8,128)(2,1)S(1)} %bitcast.4, bf16[27,16,128]{2,1,0:T(8,128)(2,1)S(1)} %bitcast.5, f32[1,128]{1,0:T(1,128)S(1)} %bitcast.6), custom_call_target="tpu_custom_call" | custom-call | tf_op jit(solution)/shard_map/pallas_call | solution.py:319
  42.8 0.0 copy-done
  42.8 2.1 %shard_map.47 = bf16[2,12,64,256]{3,2,1,0:T(8,128)(2,1)} custom-call(bf16[2,128,768]{2,1,0:T(8,128)(2,1)S(1)} %shard_map.46.hidden, bf16[27,64,128]{2,1,0:T(8,128)(2,1)S(1)} %copy-done), custom_call_target="tpu_custom_call" | custom-call | tf_op jit(solution)/shard_map/pallas_call | solution.py:360
Async XLA Ops:
  0.0 0.7 %copy-start.3 = (f32[128]{0:T(128)S(1)}, f32[128]{0:T(128)}, u32[]{:S(2)}) copy-start(f32[128]{0:T(128)} %param.6) | copy-start | bytes 1540
  0.7 1.0 %copy-start.1 = (bf16[16,16,6,128]{3,1,2,0:T(8,128)(2,1)S(1)}, bf16[16,16,6,128]{3,1,2,0:T(8,128)(2,1)}, u32[]{:S(2)}) copy-start(bf16[16,16,6,128]{3,1,2,0:T(8,128)(2,1)} %param.4) | copy-start | bytes 1179652
  1.7 0.9 %copy-start.2 = (bf16[16,27,128]{2,0,1:T(8,128)(2,1)S(1)}, bf16[16,27,128]{2,0,1:T(8,128)(2,1)}, u32[]{:S(2)}) copy-start(bf16[16,27,128]{2,0,1:T(8,128)(2,1)} %param.5) | copy-start | bytes 331780
  2.5 40.3 %copy-start = (bf16[27,64,128]{2,1,0:T(8,128)(2,1)S(1)}, bf16[27,64,128]{2,1,0:T(8,128)(2,1)}, u32[]{:S(2)}) copy-start(bf16[27,64,128]{2,1,0:T(8,128)(2,1)} %tconv.1) | copy-start | bytes 1327108

commit v3 on v2

--- a/solution.py
+++ b/solution.py
@@ -49,13 +49,19 @@
 
 
 def exchange_conv(volume, weight, bias, hidden_out, planes, weights, hidden, bias_row, entry_sem,
-                  vsend, vrecv, hsend, hrecv, wsend, rsend, wrecv, xsend, csend, crecv, esend, erecv):
+                  vsend, vrecv, osend, orecv, hsend, hrecv, psend, precv,
+                  wsend, rsend, wrecv, xsend, csend, crecv, esend, erecv):
     me = lax.axis_index("gx")
     count = lax.axis_size("gx")
     group = lax.axis_index("groups")
     chips = count // 2
     chip, core = me // 2, me % 2
+    beds = count // 4
+    bed, row = me // 4, chip % 2
+    partner = me + 1 - 2 * core
     wide_y, wide_z = volume.shape[1], volume.shape[3]
+    taps = weight.shape[0]
+    cuts = ((0, (taps + 1) // 2), ((taps + 1) // 2, taps // 2))
 
     barrier = pltpu.get_barrier_semaphore()
     for d in range(1, count):
@@ -71,9 +77,19 @@
             device_id=target, device_id_type=MESH,
         )
 
+    def arrived(at, sem):
+        pltpu.make_async_copy(at, at, sem).wait()
+
+    inner = (me > 0) & (me < count - 1)
+    outer = me - 1 + 2 * core
     own_volume = pltpu.make_async_copy(volume.at[me], planes.at[1, me], entry_sem.at[0])
     own_weight = pltpu.make_async_copy(weight, weights.at[me], entry_sem.at[1])
     own_bias = pltpu.make_async_copy(bias, bias_row, entry_sem.at[2])
+
+    def own_outer():
+        return pltpu.make_async_copy(
+            volume.at[outer], planes.at[2 * core, me], entry_sem.at[3]
+        )
 
     half = chips // 2
     place = chip % half
@@ -86,46 +102,86 @@
     def far(j):
         return (half - base) + (place + j) % half
 
-    def leads(c):
-        return (c // 2 + c) % 2 == group
-
-    def direct(j):
+    others = [mirror] + [near(j) for j in range(1, half)] + [far(j) for j in range(1, half)]
+
+    def shard(slot, q):
+        return weights.at[slot, pl.ds(*cuts[q])]
+
+    def direct(q, j):
         to = mirror if j == 0 else near(j)
-        return remote(weight, weights.at[me], wsend.at[j], wrecv.at[chip], {"gx": to * 2 + core})
-
-    def relay(j):
-        at = weights.at[mirror * 2 + core]
-        return remote(at, at, rsend.at[j], wrecv.at[mirror], {"gx": near(j) * 2 + core})
-
-    def across(c):
-        at = weights.at[c * 2 + core]
-        return remote(at, at, xsend.at[c], wrecv.at[c], {"groups": 1 - group})
-
-    def beside(c, own=False):
-        slot = c * 2 + core
-        src = weight if own else weights.at[slot]
-        return remote(src, weights.at[slot], csend.at[c], crecv.at[c], {"gx": chip * 2 + 1 - core})
+        return remote(
+            weight.at[pl.ds(*cuts[q])], shard(me, q), wsend.at[j], wrecv.at[q, chip],
+            {"gx": to * 2 + core},
+        )
+
+    def relay(q, j):
+        at = shard(mirror * 2 + core, q)
+        return remote(at, at, rsend.at[j], wrecv.at[q, mirror], {"gx": near(j) * 2 + core})
+
+    def across(q, c):
+        at = shard(c * 2 + core, q)
+        return remote(at, at, xsend.at[c], wrecv.at[q, c], {"groups": 1 - group})
+
+    def beside(q, c, own=False):
+        at = shard(c * 2 + core, q)
+        src = weight.at[pl.ds(*cuts[q])] if own else at
+        return remote(src, at, csend.at[q, c], crecv.at[q, c], {"gx": partner})
 
     def piece(d):
         to = (me + d) % count
-        return remote(volume.at[to], planes.at[1, me], vsend.at[d], vrecv.at[d], {"gx": to})
-
-    def arrived(at, sem):
-        pltpu.make_async_copy(at, at, sem).wait()
+        return remote(volume.at[to], planes.at[1, me], vsend.at[d], vrecv.at[me], {"gx": to})
+
+    def mates():
+        found = [(0, partner, 1 - core)]
+        for db in range(1, beds):
+            for cc in range(2):
+                found.append((2 * db + cc, ((bed + db) % beds) * 4 + row * 2 + cc, cc))
+        return found
+
+    def outer_piece(k, to, cc):
+        return remote(
+            volume.at[to - 1 + 2 * cc], planes.at[2 * cc, me], osend.at[k], orecv.at[me],
+            {"gx": to},
+        )
+
+    def chunk(slot, zz, yy):
+        return planes.at[slot, pl.ds(zz * 4 + yy * 2, 2)]
+
+    def to_partner(zz, yy):
+        return remote(
+            chunk(1, zz, yy), chunk(2 * core, zz, yy), psend.at[zz, yy], precv.at[zz, yy],
+            {"gx": partner},
+        )
+
+    def to_outer(zz):
+        return remote(
+            chunk(1, zz, row), chunk(2 - 2 * core, zz, row), hsend.at[zz], hrecv.at[zz],
+            {"gx": outer},
+        )
 
     order = [d for pair in zip(range(1, count // 2), range(count - 1, count // 2, -1)) for d in pair]
     order = [count // 2] + order[::-1]
-    others = [mirror] + [near(j) for j in range(1, half)] + [far(j) for j in range(1, half)]
-
-    @pl.when(leads(chip))
-    def _():
-        for j in range(half):
-            direct(j).start()
+
+    for g in range(2):
+        @pl.when(group == g)
+        def _(g=g):
+            for j in range(half):
+                direct(g, j).start()
 
     for d in order:
         piece(d).start()
-    beside(chip, True).start()
     own_volume.start()
+    for k, to, cc in mates():
+        @pl.when((to > 0) & (to < count - 1))
+        def _(k=k, to=to, cc=cc):
+            outer_piece(k, to, cc).start()
+
+    @pl.when(inner)
+    def _():
+        own_outer().start()
+
+    for q in range(2):
+        beside(q, chip, True).start()
     own_weight.start()
     own_bias.start()
 
@@ -138,52 +194,56 @@
         planes[2] = jnp.zeros(planes.shape[1:], planes.dtype)
         hidden[1] = jnp.zeros(hidden.shape[1:], hidden.dtype)
 
-    for c in others:
-        @pl.when(leads(c))
-        def _(c=c):
-            arrived(weights.at[c * 2 + core], wrecv.at[c])
-            if c is mirror:
-                for j in range(1, half):
-                    relay(j).start()
-            across(c).start()
-            beside(c).start()
+    for g in range(2):
+        @pl.when(group == g)
+        def _(g=g):
+            for i, c in enumerate(others):
+                arrived(shard(c * 2 + core, g), wrecv.at[g, c])
+                if i == 0:
+                    for j in range(1, half):
+                        relay(g, j).start()
+                across(g, c).start()
+                beside(g, c).start()
 
     own_volume.wait()
-    for d in order:
-        arrived(planes.at[1, (me + count - d) % count], vrecv.at[d])
-
-    def to_right():
-        return remote(planes.at[1], planes.at[0], hsend.at[0], hrecv.at[0], {"gx": me + 1})
-
-    def to_left():
-        return remote(planes.at[1], planes.at[2], hsend.at[1], hrecv.at[1], {"gx": me - 1})
-
-    @pl.when(me < count - 1)
-    def _():
-        to_right().start()
-
-    @pl.when(me > 0)
-    def _():
-        to_left().start()
-
-    for c in others:
-        @pl.when(jnp.logical_not(leads(c)))
-        def _(c=c):
-            arrived(weights.at[c * 2 + core], wrecv.at[c])
-            beside(c).start()
+    chunks = [((bed + db) % beds, yy) for yy in (row, 1 - row) for db in range(beds)]
+    for i, (zz, yy) in enumerate(chunks):
+        for cc in range(2):
+            src = zz * 4 + yy * 2 + cc
+
+            @pl.when(src != me)
+            def _(src=src):
+                arrived(planes.at[1, src], vrecv.at[src])
+
+        to_partner(zz, yy).start()
+        if i < beds:
+            @pl.when(inner)
+            def _(zz=zz):
+                to_outer(zz).start()
+
+    for g in range(2):
+        @pl.when(group == g)
+        def _(g=g):
+            for c in others:
+                arrived(shard(c * 2 + core, 1 - g), wrecv.at[1 - g, c])
+                beside(1 - g, c).start()
 
     own_weight.wait()
     own_bias.wait()
+
+    @pl.when(inner)
+    def _():
+        own_outer().wait()
+        for k, src, cc in mates():
+            arrived(planes.at[2 * core, src], orecv.at[src])
+        for zz in range(beds):
+            arrived(chunk(2 * core, zz, 1 - row), hrecv.at[zz])
+
+    for zz, yy in chunks:
+        arrived(chunk(2 - 2 * core, zz, yy), precv.at[zz, yy])
     for c in [chip] + others:
-        arrived(weights.at[c * 2 + 1 - core], crecv.at[c])
-
-    @pl.when(me > 0)
-    def _():
-        arrived(planes.at[0], hrecv.at[0])
-
-    @pl.when(me < count - 1)
-    def _():
-        arrived(planes.at[2], hrecv.at[1])
+        for q in range(2):
+            arrived(shard(c * 2 + 1 - core, q), crecv.at[q, c])
 
     cin = count * volume.shape[2]
     cells = [lambda y, kx=kx: planes[kx, :, y].reshape(cin, wide_z) for kx in range(3)]
@@ -201,29 +261,33 @@
 
     for d in order:
         piece(d).wait_send()
-
-    @pl.when(leads(chip))
-    def _():
-        for j in range(half):
-            direct(j).wait_send()
-        for j in range(1, half):
-            relay(j).wait_send()
-
-    beside(chip, True).wait_send()
-    for c in others:
-        @pl.when(leads(c))
-        def _(c=c):
-            across(c).wait_send()
-
-        beside(c).wait_send()
-
-    @pl.when(me < count - 1)
-    def _():
-        to_right().wait_send()
-
-    @pl.when(me > 0)
-    def _():
-        to_left().wait_send()
+    for k, to, cc in mates():
+        @pl.when((to > 0) & (to < count - 1))
+        def _(k=k, to=to, cc=cc):
+            outer_piece(k, to, cc).wait_send()
+
+    for zz, yy in chunks:
+        to_partner(zz, yy).wait_send()
+
+    @pl.when(inner)
+    def _():
+        for zz in range(beds):
+            to_outer(zz).wait_send()
+
+    for g in range(2):
+        @pl.when(group == g)
+        def _(g=g):
+            for j in range(half):
+                direct(g, j).wait_send()
+            for j in range(1, half):
+                relay(g, j).wait_send()
+            for c in others:
+                across(g, c).wait_send()
+
+    for q in range(2):
+        beside(q, chip, True).wait_send()
+        for c in others:
+            beside(q, c).wait_send()
 
     @pl.when(me < count - 1)
     def _():
@@ -326,11 +390,11 @@
             pltpu.VMEM((count,) + weight.shape, jnp.bfloat16),
             pltpu.VMEM((2, cout, lanes), jnp.bfloat16),
             pltpu.VMEM((1, cout), jnp.float32),
-            dma((3,)),
-            dma((count,)), dma((count,)),
-            dma((2,)), dma((2,)),
-            dma((chips,)), dma((chips,)), dma((chips,)),
-            dma((chips,)), dma((chips,)), dma((chips,)),
+            dma((4,)),
+            dma((count,)), dma((count,)), dma((chips,)), dma((count,)),
+            dma((count // 4,)), dma((count // 4,)), dma((count // 4, 2)), dma((count // 4, 2)),
+            dma((chips,)), dma((chips,)), dma((2, chips)), dma((chips,)),
+            dma((2, chips)), dma((2, chips)),
             dma(()), dma(()),
         ],
         compiler_params=pltpu.CompilerParams(

time: 45.1 us -> 39.8 us (0.88)
  Pallas kernels: 42.3 us -> 37 us
    pallas_call x1, Pallas kernels: 40.2 us -> 34.9 us  [remote_hidden(): pl.pallas_call(exchange_conv, out_shape=jax.ShapeDtypeStruct((2, cout, la...]
where the time goes in v3:
time: 39.8 us; the launch traced here: 39.6 us
  Pallas kernels  37 us (93%)
  local copies, waits for them, and re-layouts  2.55 us (6%)
    pallas_call x1, Pallas kernels, remote_hidden(): pl.pallas_call(exchange_conv, out_shape=jax.ShapeDtypeStruct((2, cout, la...  34.9 us
    unnamed x8, local copies, waits for them, and re-layouts  2.55 us
    pallas_call x1, Pallas kernels, per_device(): outs = [tconv(planes, tconv_weight) for planes in hidden]  2.09 us

profile of v3, /device:TPU:9, one launch (start us, length us, event | category | flops | bytes accessed | tf_op | source)
XLA Modules:
  0.0 39.6 jit_solution(3319353055608098100)
XLA Ops:
  0.0 0.0 copy-start.3
  0.0 0.7 %copy-done.3 = f32[128]{0:T(128)S(1)} copy-done((f32[128]{0:T(128)S(1)}, f32[128]{0:T(128)}, u32[]{:S(2)}) %copy-start.3) | copy-done | bytes 536
  0.7 0.0 copy-start.1
  0.7 1.0 %copy-done.1 = bf16[16,16,6,128]{3,1,2,0:T(8,128)(2,1)S(1)} copy-done((bf16[16,16,6,128]{3,1,2,0:T(8,128)(2,1)S(1)}, bf16[16,16,6,128]{3,1,2,0:T(8,128)(2,1)}, u32[]{:S(2)}) %copy-start.1) | copy-done | bytes 393240
  1.7 0.0 copy-start.2
  1.7 0.9 %copy-done.2 = bf16[16,27,128]{2,0,1:T(8,128)(2,1)S(1)} copy-done((bf16[16,27,128]{2,0,1:T(8,128)(2,1)S(1)}, bf16[16,27,128]{2,0,1:T(8,128)(2,1)}, u32[]{:S(2)}) %copy-start.2) | copy-done | bytes 110616
  2.5 0.0 copy-start
  2.6 34.9 %shard_map.46.hidden = bf16[2,128,768]{2,1,0:T(8,128)(2,1)S(1)} custom-call(bf16[16,6,16,128]{3,2,1,0:T(8,128)(2,1)S(1)} %bitcast.4, bf16[27,16,128]{2,1,0:T(8,128)(2,1)S(1)} %bitcast.5, f32[1,128]{1,0:T(1,128)S(1)} %bitcast.6), custom_call_target="tpu_custom_call" | custom-call | tf_op jit(solution)/shard_map/pallas_call | solution.py:383
  37.5 0.0 copy-done
  37.5 2.1 %shard_map.47 = bf16[2,12,64,256]{3,2,1,0:T(8,128)(2,1)} custom-call(bf16[2,128,768]{2,1,0:T(8,128)(2,1)S(1)} %shard_map.46.hidden, bf16[27,64,128]{2,1,0:T(8,128)(2,1)S(1)} %copy-done), custom_call_target="tpu_custom_call" | custom-call | tf_op jit(solution)/shard_map/pallas_call | solution.py:424
Async XLA Ops:
  0.0 0.7 %copy-start.3 = (f32[128]{0:T(128)S(1)}, f32[128]{0:T(128)}, u32[]{:S(2)}) copy-start(f32[128]{0:T(128)} %param.6) | copy-start | bytes 1540
  0.7 1.0 %copy-start.1 = (bf16[16,16,6,128]{3,1,2,0:T(8,128)(2,1)S(1)}, bf16[16,16,6,128]{3,1,2,0:T(8,128)(2,1)}, u32[]{:S(2)}) copy-start(bf16[16,16,6,128]{3,1,2,0:T(8,128)(2,1)} %param.4) | copy-start | bytes 1179652
  1.7 0.9 %copy-start.2 = (bf16[16,27,128]{2,0,1:T(8,128)(2,1)S(1)}, bf16[16,27,128]{2,0,1:T(8,128)(2,1)}, u32[]{:S(2)}) copy-start(bf16[16,27,128]{2,0,1:T(8,128)(2,1)} %param.5) | copy-start | bytes 331780
  2.5 34.9 %copy-start = (bf16[27,64,128]{2,1,0:T(8,128)(2,1)S(1)}, bf16[27,64,128]{2,1,0:T(8,128)(2,1)}, u32[]{:S(2)}) copy-start(bf16[27,64,128]{2,1,0:T(8,128)(2,1)} %tconv.1) | copy-start | bytes 1327108

commit v4 on v3

--- a/solution.py
+++ b/solution.py
@@ -48,7 +48,7 @@
     return jnp.maximum(jnp.concatenate(rows, axis=1), 0.0).astype(jnp.bfloat16)
 
 
-def exchange_conv(volume, weight, bias, hidden_out, planes, weights, hidden, bias_row, entry_sem,
+def exchange_conv(volume, weight, bias, tconv, out, planes, weights, hidden, bias_row, tconv_rows, entry_sem,
                   vsend, vrecv, osend, orecv, hsend, hrecv, psend, precv,
                   wsend, rsend, wrecv, xsend, csend, crecv, esend, erecv):
     me = lax.axis_index("gx")
@@ -86,6 +86,8 @@
     own_weight = pltpu.make_async_copy(weight, weights.at[me], entry_sem.at[1])
     own_bias = pltpu.make_async_copy(bias, bias_row, entry_sem.at[2])
 
+    own_tconv = pltpu.make_async_copy(tconv, tconv_rows, entry_sem.at[4])
+
     def own_outer():
         return pltpu.make_async_copy(
             volume.at[outer], planes.at[2 * core, me], entry_sem.at[3]
@@ -184,6 +186,7 @@
         beside(q, chip, True).start()
     own_weight.start()
     own_bias.start()
+    own_tconv.start()
 
     @pl.when(me == 0)
     def _():
@@ -259,6 +262,9 @@
     def _():
         edge().start()
 
+    own_tconv.wait()
+    decode(hidden, tconv_rows, out, 0)
+
     for d in order:
         piece(d).wait_send()
     for k, to, cc in mates():
@@ -297,7 +303,7 @@
     def _():
         edge().wait_send()
 
-    hidden_out[...] = hidden[...]
+    decode(hidden, tconv_rows, out, 1)
 
 
 def local_conv(planes, weight, bias, hidden_out):
@@ -307,11 +313,15 @@
 
 
 def transposed(hidden, tconv, out):
+    decode(hidden, tconv, out, 0)
+    decode(hidden, tconv, out, 1)
+
+
+def decode(hidden, tconv, out, pu):
     wide_z = out.shape[3] // 2
     wide_y = out.shape[1] // 2
     cup = tconv.shape[1]
     cout = tconv.shape[2]
-    here, after = hidden[0], hidden[1]
 
     def down(x):
         return jnp.concatenate([x[:, wide_z:], jnp.zeros_like(x[:, :wide_z])], axis=1)
@@ -325,29 +335,29 @@
     spread = jnp.where(
         col == jnp.where(row < wide_z, 2 * row, 2 * (row - wide_z) + 1), 1.0, 0.0
     ).astype(jnp.bfloat16)
-    x_options = (((1, here),), ((2, here), (0, after)))
-    for pu in range(2):
-        for pv in range(2):
-            left, right = [], []
-            for kx, field in x_options[pu]:
-                for ky, shifted in (((1, False),), ((2, False), (0, True)))[pv]:
-                    left.append(taps(kx, ky))
-                    right.append(down(field) if shifted else field)
-            product = jnp.dot(
-                jnp.concatenate(left, axis=1), jnp.concatenate(right, axis=0),
-                preferred_element_type=jnp.float32,
-            )
-            pairs = []
-            for y in range(wide_y):
-                part = product[:, y * wide_z : (y + 1) * wide_z]
-                even = part[cup : 2 * cup]
-                odd = part[2 * cup :] + shift_down(part[:cup])
-                pairs.append(jnp.concatenate([even, odd], axis=1).astype(jnp.bfloat16))
-            mixed = jnp.dot(
-                jnp.concatenate(pairs, axis=0), spread, preferred_element_type=jnp.float32
-            ).astype(jnp.bfloat16)
-            for y in range(wide_y):
-                out[pu, 2 * y + pv] = mixed[y * cup : (y + 1) * cup]
+    x_options = ((1, 0),) if pu == 0 else ((2, 0), (0, 1))
+    for pv in range(2):
+        left, right = [], []
+        for kx, at in x_options:
+            field = hidden[at]
+            for ky, shifted in (((1, False),), ((2, False), (0, True)))[pv]:
+                left.append(taps(kx, ky))
+                right.append(down(field) if shifted else field)
+        product = jnp.dot(
+            jnp.concatenate(left, axis=1), jnp.concatenate(right, axis=0),
+            preferred_element_type=jnp.float32,
+        )
+        pairs = []
+        for y in range(wide_y):
+            part = product[:, y * wide_z : (y + 1) * wide_z]
+            even = part[cup : 2 * cup]
+            odd = part[2 * cup :] + shift_down(part[:cup])
+            pairs.append(jnp.concatenate([even, odd], axis=1).astype(jnp.bfloat16))
+        mixed = jnp.dot(
+            jnp.concatenate(pairs, axis=0), spread, preferred_element_type=jnp.float32
+        ).astype(jnp.bfloat16)
+        for y in range(wide_y):
+            out[pu, 2 * y + pv] = mixed[y * cup : (y + 1) * cup]
 
 
 def native_hidden(volume, conv_weight, bias):
@@ -372,7 +382,7 @@
     return [jnp.stack(hidden[r : r + 2]) for r in range(rows)]
 
 
-def remote_hidden(volume, conv_weight, bias):
+def remote_decoded(volume, conv_weight, bias, tconv_weight, shape):
     count = lax.axis_size("gx")
     chips = count // 2
     cells = jnp.transpose(volume, (0, 2, 1, 3))
@@ -380,17 +390,18 @@
     cout = weight.shape[2]
     lanes = cells.shape[1] * cells.shape[3]
     dma = pltpu.SemaphoreType.DMA
-    hidden = pl.pallas_call(
+    return pl.pallas_call(
         exchange_conv,
-        out_shape=jax.ShapeDtypeStruct((2, cout, lanes), jnp.bfloat16),
-        in_specs=[HBM, HBM, HBM],
+        out_shape=shape,
+        in_specs=[HBM] * 4,
         out_specs=VMEM,
         scratch_shapes=[
             pltpu.VMEM((3, count) + cells.shape[1:], jnp.bfloat16),
             pltpu.VMEM((count,) + weight.shape, jnp.bfloat16),
             pltpu.VMEM((2, cout, lanes), jnp.bfloat16),
             pltpu.VMEM((1, cout), jnp.float32),
-            dma((4,)),
+            pltpu.VMEM(tconv_weight.shape, jnp.bfloat16),
+            dma((5,)),
             dma((count,)), dma((count,)), dma((chips,)), dma((count,)),
             dma((count // 4,)), dma((count // 4,)), dma((count // 4, 2)), dma((count // 4, 2)),
             dma((chips,)), dma((chips,)), dma((2, chips)), dma((chips,)),
@@ -398,10 +409,9 @@
             dma(()), dma(()),
         ],
         compiler_params=pltpu.CompilerParams(
-            collective_id=0, has_side_effects=True, vmem_limit_bytes=40 << 20
+            collective_id=0, has_side_effects=True, vmem_limit_bytes=60 << 20
         ),
-    )(cells, weight, bias.reshape(1, cout))
-    return [hidden]
+    )(cells, weight, bias.reshape(1, cout), tconv_weight)
 
 
 def per_device(volume, conv_weight, conv_bias, tconv_weight):
@@ -412,17 +422,20 @@
         rows == 1 and count == 16 and lax.axis_size("groups") == 2
         and volume.shape[1] % 16 == 0
     )
-    hidden = (remote_hidden if suited else native_hidden)(volume, conv_weight, bias)
     cup = tconv_weight.shape[1]
     shape = jax.ShapeDtypeStruct(
         (2, 2 * volume.shape[2], cup, 2 * volume.shape[3]), jnp.bfloat16
     )
-    tconv = pl.pallas_call(
-        transposed, out_shape=shape, in_specs=[VMEM] * 2, out_specs=VMEM,
-        compiler_params=pltpu.CompilerParams(vmem_limit_bytes=40 << 20),
-    )
-    outs = [tconv(planes, tconv_weight) for planes in hidden]
-    out = outs[0] if len(outs) == 1 else jnp.concatenate(outs, axis=0)
+    if suited:
+        out = remote_decoded(volume, conv_weight, bias, tconv_weight, shape)
+    else:
+        tconv = pl.pallas_call(
+            transposed, out_shape=shape, in_specs=[VMEM] * 2, out_specs=VMEM,
+            compiler_params=pltpu.CompilerParams(vmem_limit_bytes=40 << 20),
+        )
+        hidden = native_hidden(volume, conv_weight, bias)
+        outs = [tconv(planes, tconv_weight) for planes in hidden]
+        out = outs[0] if len(outs) == 1 else jnp.concatenate(outs, axis=0)
     return jnp.transpose(out, (0, 2, 1, 3))
 
 

time: 39.8 us -> 39.5 us (level)
  local copies, waits for them, and re-layouts: 2.55 us -> 2.09 us
    unnamed x8 -> x1, local copies, waits for them, and re-layouts: 2.55 us -> 2.09 us
    pallas_call x2 -> x1, Pallas kernels: 37 us -> 37.3 us  [remote_decoded(): pl.pallas_call(exchange_conv, out_shape=shape, in_specs=[HBM] * 4, out_sp...]
where the time goes in v4:
time: 39.5 us; the launch traced here: 39.4 us
  Pallas kernels  37.3 us (94%)
  local copies, waits for them, and re-layouts  2.09 us (5%)
    pallas_call x1, Pallas kernels, remote_decoded(): pl.pallas_call(exchange_conv, out_shape=shape, in_specs=[HBM] * 4, out_sp...  37.3 us
    unnamed x1, local copies, waits for them, and re-layouts  2.09 us

profile of v4, /device:TPU:9, one launch (start us, length us, event | category | flops | bytes accessed | tf_op | source)
XLA Modules:
  0.0 39.4 jit_solution(11591086693965739982)
XLA Ops:
  0.0 37.3 %shard_map.46 = bf16[2,12,64,256]{3,2,1,0:T(8,128)(2,1)} custom-call(bf16[16,6,16,128]{3,2,1,0:T(8,128)(2,1)} %bitcast.5, bf16[27,16,128]{2,1,0:T(8,128)(2,1)} %bitcast.6, f32[1,128]{1,0:T(1,128)} %bitcast.7, bf16[27,64,128]{2,1,0:T(8,128)(2,1)} %tconv.1), custom_call_target="tpu_custom_call" | custom-call | tf_op jit(solution)/shard_map/pallas_call | solution.py:393
  37.3 2.1 %copy.6 = bf16[2,64,12,256]{3,1,2,0:T(8,128)(2,1)} copy(bf16[2,64,12,256]{3,1,2,0:T(8,128)(2,1)} %bitcast.4) | data formatting | bytes 1572864

commit v5 on v3

--- a/solution.py
+++ b/solution.py
@@ -168,14 +168,7 @@
             for j in range(half):
                 direct(g, j).start()
 
-    for d in order:
-        piece(d).start()
     own_volume.start()
-    for k, to, cc in mates():
-        @pl.when((to > 0) & (to < count - 1))
-        def _(k=k, to=to, cc=cc):
-            outer_piece(k, to, cc).start()
-
     @pl.when(inner)
     def _():
         own_outer().start()
@@ -202,8 +195,15 @@
                 if i == 0:
                     for j in range(1, half):
                         relay(g, j).start()
+                    for d in order:
+                        piece(d).start()
                 across(g, c).start()
                 beside(g, c).start()
+
+    for k, to, cc in mates():
+        @pl.when((to > 0) & (to < count - 1))
+        def _(k=k, to=to, cc=cc):
+            outer_piece(k, to, cc).start()
 
     own_volume.wait()
     chunks = [((bed + db) % beds, yy) for yy in (row, 1 - row) for db in range(beds)]
@@ -398,7 +398,7 @@
             dma(()), dma(()),
         ],
         compiler_params=pltpu.CompilerParams(
-            collective_id=0, has_side_effects=True, vmem_limit_bytes=40 << 20
+            collective_id=0, has_side_effects=True, vmem_limit_bytes=60 << 20
         ),
     )(cells, weight, bias.reshape(1, cout))
     return [hidden]

time: 39.8 us -> 36.4 us (0.915)
  Pallas kernels: 37 us -> 35.3 us
  local copies, waits for them, and re-layouts: 2.55 us -> 0.99 us
    pallas_call x1, Pallas kernels: 34.9 us -> 33.2 us  [remote_hidden(): pl.pallas_call(exchange_conv, out_shape=jax.ShapeDtypeStruct((2, cout, la...]
    unnamed x8 -> x4, local copies, waits for them, and re-layouts: 2.55 us -> 0.99 us
where the time goes in v5:
time: 36.4 us; the launch traced here: 36.3 us
  Pallas kernels  35.3 us (97%)
  local copies, waits for them, and re-layouts  0.99 us (3%)
    pallas_call x1, Pallas kernels, remote_hidden(): pl.pallas_call(exchange_conv, out_shape=jax.ShapeDtypeStruct((2, cout, la...  33.2 us
    pallas_call x1, Pallas kernels, per_device(): outs = [tconv(planes, tconv_weight) for planes in hidden]  2.09 us
    unnamed x4, local copies, waits for them, and re-layouts  0.99 us

profile of v5, /device:TPU:9, one launch (start us, length us, event | category | flops | bytes accessed | tf_op | source)
XLA Modules:
  0.0 36.3 jit_solution(15093432922483046429)
XLA Ops:
  0.0 0.0 copy-start.1
  0.0 33.2 %shard_map.46.hidden = bf16[2,128,768]{2,1,0:T(8,128)(2,1)} custom-call(bf16[16,6,16,128]{3,2,1,0:T(8,128)(2,1)} %bitcast.4, bf16[27,16,128]{2,1,0:T(8,128)(2,1)} %bitcast.5, f32[1,128]{1,0:T(1,128)} %bitcast.6), custom_call_target="tpu_custom_call" | custom-call | tf_op jit(solution)/shard_map/pallas_call | solution.py:383
  33.2 0.0 copy-done.1
  33.2 0.0 copy-start
  33.2 1.0 %copy-done = bf16[2,128,768]{2,1,0:T(8,128)(2,1)S(1)} copy-done((bf16[2,128,768]{2,1,0:T(8,128)(2,1)S(1)}, bf16[2,128,768]{2,1,0:T(8,128)(2,1)}, u32[]{:S(2)}) %copy-start) | copy-done | bytes 393240
  34.2 2.1 %shard_map.47 = bf16[2,12,64,256]{3,2,1,0:T(8,128)(2,1)} custom-call(bf16[2,128,768]{2,1,0:T(8,128)(2,1)S(1)} %copy-done, bf16[27,64,128]{2,1,0:T(8,128)(2,1)S(1)} %copy-done.1), custom_call_target="tpu_custom_call" | custom-call | tf_op jit(solution)/shard_map/pallas_call | solution.py:424
Async XLA Ops:
  0.0 33.2 %copy-start.1 = (bf16[27,64,128]{2,1,0:T(8,128)(2,1)S(1)}, bf16[27,64,128]{2,1,0:T(8,128)(2,1)}, u32[]{:S(2)}) copy-start(bf16[27,64,128]{2,1,0:T(8,128)(2,1)} %tconv.1) | copy-start | bytes 1327108
  33.2 1.0 %copy-start = (bf16[2,128,768]{2,1,0:T(8,128)(2,1)S(1)}, bf16[2,128,768]{2,1,0:T(8,128)(2,1)}, u32[]{:S(2)}) copy-start(bf16[2,128,768]{2,1,0:T(8,128)(2,1)} %shard_map.46.hidden) | copy-start | bytes 1179652

commit v6 on v5

--- a/solution.py
+++ b/solution.py
@@ -21,7 +21,8 @@
     return jnp.where(lane == size - 1, 0.0, pltpu.roll(block, size - 1, axis=1))
 
 
-def conv_hidden(planes, wide_y, wide_z, tap, bias):
+def conv_hidden(planes, wide_y, wide_z, tap, bias, first=0, span=None):
+    span = span or wide_y
     zero = jnp.zeros_like(planes[0](0))
     total = None
     for kx in range(3):
@@ -30,14 +31,14 @@
         )
         for ky in range(3):
             weight = jnp.concatenate([tap(kx * 9 + ky * 3 + kz) for kz in range(3)], axis=1)
-            cells = padded[:, ky * wide_z : (ky + wide_y) * wide_z]
+            cells = padded[:, (ky + first) * wide_z : (ky + first + span) * wide_z]
             term = lax.dot_general(
                 weight, cells, (((0,), (0,)), ((), ())), preferred_element_type=jnp.float32
             )
             total = term if total is None else total + term
     cout = total.shape[0] // 3
     rows = []
-    for y in range(wide_y):
+    for y in range(span):
         part = total[:, y * wide_z : (y + 1) * wide_z]
         rows.append(
             part[cout : 2 * cout]
@@ -247,17 +248,26 @@
 
     cin = count * volume.shape[2]
     cells = [lambda y, kx=kx: planes[kx, :, y].reshape(cin, wide_z) for kx in range(3)]
-    hidden[0] = conv_hidden(
-        cells, wide_y, wide_z, lambda t: weights[:, t].reshape(cin, weights.shape[3]),
-        jnp.transpose(jnp.broadcast_to(bias_row[...], (wide_z, bias_row.shape[1]))),
-    )
-
-    def edge():
-        return remote(hidden.at[0], hidden.at[1], esend, erecv, {"gx": me - 1})
-
-    @pl.when(me > 0)
-    def _():
-        edge().start()
+    bias_cells = jnp.transpose(jnp.broadcast_to(bias_row[...], (wide_z, bias_row.shape[1])))
+    span = wide_y // 2 if wide_y % 2 == 0 else wide_y
+    parts = wide_y // span
+
+    def edge(i):
+        lanes = pl.ds(i * span * wide_z, span * wide_z)
+        return remote(
+            hidden.at[0, :, lanes], hidden.at[1, :, lanes], esend.at[i], erecv.at[i],
+            {"gx": me - 1},
+        )
+
+    for i in range(parts):
+        hidden[0, :, pl.ds(i * span * wide_z, span * wide_z)] = conv_hidden(
+            cells, wide_y, wide_z, lambda t: weights[:, t].reshape(cin, weights.shape[3]),
+            bias_cells, i * span, span,
+        )
+
+        @pl.when(me > 0)
+        def _(i=i):
+            edge(i).start()
 
     for d in order:
         piece(d).wait_send()
@@ -291,11 +301,13 @@
 
     @pl.when(me < count - 1)
     def _():
-        arrived(hidden.at[1], erecv)
+        for i in range(parts):
+            arrived(hidden.at[1, :, pl.ds(i * span * wide_z, span * wide_z)], erecv.at[i])
 
     @pl.when(me > 0)
     def _():
-        edge().wait_send()
+        for i in range(parts):
+            edge(i).wait_send()
 
     hidden_out[...] = hidden[...]
 
@@ -395,7 +407,7 @@
             dma((count // 4,)), dma((count // 4,)), dma((count // 4, 2)), dma((count // 4, 2)),
             dma((chips,)), dma((chips,)), dma((2, chips)), dma((chips,)),
             dma((2, chips)), dma((2, chips)),
-            dma(()), dma(()),
+            dma((2,)), dma((2,)),
         ],
         compiler_params=pltpu.CompilerParams(
             collective_id=0, has_side_effects=True, vmem_limit_bytes=60 << 20

time: 36.4 us -> 36.1 us (level)
  no operation moved by 1% of the time
where the time goes in v6:
time: 36.1 us; the launch traced here: 36 us
  Pallas kernels  35 us (97%)
  local copies, waits for them, and re-layouts  0.99 us (3%)
    pallas_call x1, Pallas kernels, remote_hidden(): pl.pallas_call(exchange_conv, out_shape=jax.ShapeDtypeStruct((2, cout, la...  32.9 us
    pallas_call x1, Pallas kernels, per_device(): outs = [tconv(planes, tconv_weight) for planes in hidden]  2.09 us
    unnamed x4, local copies, waits for them, and re-layouts  0.99 us

profile of v6, /device:TPU:9, one launch (start us, length us, event | category | flops | bytes accessed | tf_op | source)
XLA Modules:
  0.0 36.0 jit_solution(8921620193867022918)
XLA Ops:
  0.0 0.0 copy-start.1
  0.0 32.9 %shard_map.46.hidden = bf16[2,128,768]{2,1,0:T(8,128)(2,1)} custom-call(bf16[16,6,16,128]{3,2,1,0:T(8,128)(2,1)} %bitcast.4, bf16[27,16,128]{2,1,0:T(8,128)(2,1)} %bitcast.5, f32[1,128]{1,0:T(1,128)} %bitcast.6), custom_call_target="tpu_custom_call" | custom-call | tf_op jit(solution)/shard_map/pallas_call | solution.py:395
  32.9 0.0 copy-done.1
  32.9 0.0 copy-start
  32.9 1.0 %copy-done = bf16[2,128,768]{2,1,0:T(8,128)(2,1)S(1)} copy-done((bf16[2,128,768]{2,1,0:T(8,128)(2,1)S(1)}, bf16[2,128,768]{2,1,0:T(8,128)(2,1)}, u32[]{:S(2)}) %copy-start) | copy-done | bytes 393240
  33.9 2.1 %shard_map.47 = bf16[2,12,64,256]{3,2,1,0:T(8,128)(2,1)} custom-call(bf16[2,128,768]{2,1,0:T(8,128)(2,1)S(1)} %copy-done, bf16[27,64,128]{2,1,0:T(8,128)(2,1)S(1)} %copy-done.1), custom_call_target="tpu_custom_call" | custom-call | tf_op jit(solution)/shard_map/pallas_call | solution.py:436
Async XLA Ops:
  0.0 32.9 %copy-start.1 = (bf16[27,64,128]{2,1,0:T(8,128)(2,1)S(1)}, bf16[27,64,128]{2,1,0:T(8,128)(2,1)}, u32[]{:S(2)}) copy-start(bf16[27,64,128]{2,1,0:T(8,128)(2,1)} %tconv.1) | copy-start | bytes 1327108
  32.9 1.0 %copy-start = (bf16[2,128,768]{2,1,0:T(8,128)(2,1)S(1)}, bf16[2,128,768]{2,1,0:T(8,128)(2,1)}, u32[]{:S(2)}) copy-start(bf16[2,128,768]{2,1,0:T(8,128)(2,1)} %shard_map.46.hidden) | copy-start | bytes 1179652
